TPU v7x, 512 devices: a whole 4x4x16 slice. The times are simulated.
512 devices in a mesh: loop: 64 (over z, x_hi, core), narrow: 8 (over x_lo, y).
Axes of the slice: x: 4 (x_hi: 2, x_lo: 2; x = x_hi * 2 + x_lo), y: 4, z: 16, core: 2. Of those that a mesh axis runs over, the one named last changes fastest.
Arguments:
- tokens: bfloat16 [1024, 8192], P('loop', 'narrow'), may hold values from -6 to 6
- gate_weight: bfloat16 [8192, 28672], P('narrow', 'loop'), may hold values from -0.0625 to 0.0625
- up_weight: bfloat16 [8192, 28672], P('narrow', 'loop'), may hold values from -0.0625 to 0.0625
- down_weight: bfloat16 [28672, 8192], P('loop', 'narrow'), may hold values from -0.03125 to 0.03125
Outputs:
- mixed: bfloat16 [1024, 8192], P('loop', 'narrow')
All inputs are finite; a program needn't handle non-finite values.
Results may differ from a plain program's by a relative error of at most 0.0049.
Values may be sent and summed in bfloat16 or wider, within the bound.
No kernel may reach another device: no remote copies, remote signals or barrier semaphores. Data moves between devices by JAX's collectives and lax.ppermute only.
A program may use at most 64 MiB of HBM per device.

v0:
```python
import jax
import jax.numpy as jnp
from jax import lax
from jax.sharding import PartitionSpec as P


def shards(tokens, gate_weight, up_weight, down_weight):
    width = gate_weight.shape[1]
    block_rows = lax.all_gather(tokens, "loop", axis=0, tiled=True)
    partial_sums = jnp.concatenate(
        (
            jnp.dot(block_rows, gate_weight, preferred_element_type=jnp.float32),
            jnp.dot(block_rows, up_weight, preferred_element_type=jnp.float32),
        ),
        axis=1,
    )
    totals = lax.psum(partial_sums, "narrow")
    hidden = (jax.nn.silu(totals[:, :width]) * totals[:, width:]).astype(jnp.bfloat16)
    mixed = lax.psum_scatter(
        jnp.dot(hidden, down_weight, preferred_element_type=jnp.float32),
        "loop",
        scatter_dimension=0,
        tiled=True,
    )
    return mixed.astype(jnp.bfloat16)


def solution(mesh):
    return jax.shard_map(
        shards,
        mesh=mesh,
        in_specs=(
            P("loop", "narrow"),
            P("narrow", "loop"),
            P("narrow", "loop"),
            P("loop", "narrow"),
        ),
        out_specs=P("loop", "narrow"),
        check_vma=False,
    )
```

profile of v0, /device:TPU:8, one launch (start us, length us, event | category | flops | bytes accessed | tf_op | source)
XLA Modules:
  0.0 507.0 jit_solution(5028401805543478411)
XLA Ops:
  6.5 0.0 copy-start
  6.5 0.0 all-gather.2.cloned.1.call-start
  6.5 0.7 all-gather.2.cloned.1.call-update
  7.3 0.0 copy-start.2
  7.3 0.0 all-reduce.2.cloned.1.call-start
  7.3 151.5 %all-gather.2.cloned.1.call-done = bf16[1024,1024]{1,0:T(8,128)(2,1)} async-done(((bf16[16,1024]{1,0:T(8,128)(2,1)}), bf16[1024,1024]{1,0:T(8,128)(2,1)}) %all-gather.2.cloned.1.call-update) | async-done | bytes 2097168 | tf_op jit(solution)/shard_map/all_gather | solution.py:9
  158.8 0.0 copy-start.1
  158.8 3.1 fusion.6
  162.0 0.0 copy-done.2
  162.0 0.0 copy-done.1
  162.0 1.2 fusion.5
  163.1 2.3 pad_maximum_fusion
  165.4 0.0 all-reduce.2.cloned.1.call-update
  165.4 0.0 reduce-scatter.2.cloned.1.call-start
  165.5 104.9 %all-reduce.2.cloned.1.call-done = f32[1024,896]{0,1:T(8,128)} async-done(((f32[1024,896]{0,1:T(8,128)}), f32[1024,896]{0,1:T(8,128)}) %all-reduce.2.cloned.1.call-update) | async-done | bytes 3670032 | tf_op jit(solution)/shard_map/psum | solution.py:17
  270.4 0.0 copy-done
  270.4 5.3 %fusion.1 = f32[1024,1024]{1,0:T(8,128)} fusion(bf16[448,1024]{1,0:T(8,128)(2,1)S(1)} %copy-done, f32[1024,896]{0,1:T(8,128)} %all-reduce.2.cloned.1.call-done), kind=kOutput, calls=%fused_computation.3 | convolution fusion | flops 942276608 | bytes 8781824 | tf_op jit(solution)/shard_map/dot_general | solution.py:20
  275.7 0.0 reduce-scatter.2.cloned.1.call-update
  275.8 223.2 %reduce-scatter.2.cloned.1.call-done = f32[16,1024]{1,0:T(8,128)} async-done(((f32[1024,1024]{1,0:T(8,128)}), f32[16,1024]{1,0:T(8,128)}) %reduce-scatter.2.cloned.1.call-update) | async-done | bytes 65552 | tf_op jit(solution)/shard_map/reduce_scatter | solution.py:19
  499.0 1.5 convert_element_type.7
Async XLA Ops:
  6.5 263.9 %copy-start = (bf16[448,1024]{1,0:T(8,128)(2,1)S(1)}, bf16[448,1024]{1,0:T(8,128)(2,1)}, u32[]{:S(2)}) copy-start(bf16[448,1024]{1,0:T(8,128)(2,1)} %param.7) | copy-start | bytes 2752516
  6.5 152.3 %all-gather.2.cloned.1.call-start = ((), (), s32[]{:S(2)}) async-start(), calls=%async_computation.1 | async-start | bytes 2129920 | tf_op jit(solution)/shard_map/all_gather | solution.py:9
  7.3 154.7 %copy-start.2 = (bf16[1024,448]{0,1:T(8,128)(2,1)S(1)}, bf16[1024,448]{0,1:T(8,128)(2,1)}, u32[]{:S(2)}) copy-start(bf16[1024,448]{0,1:T(8,128)(2,1)} %param.5) | copy-start | bytes 2752516
  7.3 263.1 %all-reduce.2.cloned.1.call-start = ((), (), s32[]{:S(2)}) async-start(), calls=%async_computation.2 | async-start | bytes 7340032 | tf_op jit(solution)/shard_map/psum | solution.py:17
  158.8 3.1 copy-start.1
  165.4 333.5 %reduce-scatter.2.cloned.1.call-start = ((), (), s32[]{:S(2)}) async-start(), calls=%async_computation.3 | async-start | bytes 4259840 | tf_op jit(solution)/shard_map/reduce_scatter | solution.py:19
Sparse Core Ops, SparseCore 0:
  10.7 148.1 all-gather.1
  165.6 104.7 all-reduce.1
  275.9 223.0 reduce-scatter.1
where the time goes:
time: 507 us
  waiting for transfers between devices  480 us (95%)
  between operations  13.1 us (3%)
  matrix products  9.59 us (2%)
    reduce_scatter x1, waiting for transfers between devices, shards(): lax.psum_scatter(jnp.dot(hidden, down_weight, preferred_element_type=jnp....  223 us
    all_gather x1, waiting for transfers between devices, shards(): block_rows = lax.all_gather(tokens, 'loop', axis=0, tiled=True)  152 us
    psum x1, waiting for transfers between devices, shards(): totals = lax.psum(partial_sums, 'narrow')  105 us
  transfers between devices with their start and end apart: 3, of which 3 were waited for; matrix products, arithmetic and copies ran while one was open for 0% of the time, Pallas kernels for 0%

commit v1 on v0

--- a/solution.py
+++ b/solution.py
@@ -6,7 +6,9 @@
 
 def shards(tokens, gate_weight, up_weight, down_weight):
     width = gate_weight.shape[1]
-    block_rows = lax.all_gather(tokens, "loop", axis=0, tiled=True)
+    block_rows = jnp.concatenate(
+        lax.all_to_all(jnp.stack([tokens] * lax.axis_size("loop")), "loop", 0, 0), axis=0
+    )
     partial_sums = jnp.concatenate(
         (
             jnp.dot(block_rows, gate_weight, preferred_element_type=jnp.float32),

time: 507 us -> 471 us (0.929)
  waiting for transfers between devices: 480 us -> 325 us
  blocking collectives: 0 us -> 120 us
    all_gather x1 -> x0, waiting for transfers between devices: 152 us -> none  [shards(): block_rows = lax.all_gather(tokens, 'loop', axis=0, tiled=True)]
    all_to_all x0 -> x1, blocking collectives: none -> 120 us  [shards(): lax.all_to_all(jnp.stack([tokens] * lax.axis_size('loop')), 'loop', 0, 0)]
  transfers between devices with their start and end apart: 3 -> 2, of which waited for: 3 -> 2; matrix products, arithmetic and copies ran while one was open for 0% -> 0% of each run, Pallas kernels for 0% -> 0%
where the time goes in v1:
time: 471 us; the launch traced here: 470 us
  waiting for transfers between devices  325 us (69%)
  blocking collectives  120 us (25%)
  between operations  13.4 us (3%)
  matrix products  7.62 us (2%)
    reduce_scatter x1, waiting for transfers between devices, shards(): lax.psum_scatter(jnp.dot(hidden, down_weight, preferred_element_type=jnp....  223 us
    all_to_all x1, blocking collectives, shards(): lax.all_to_all(jnp.stack([tokens] * lax.axis_size('loop')), 'loop', 0, 0)  120 us
    psum x1, waiting for transfers between devices, shards(): totals = lax.psum(partial_sums, 'narrow')  102 us
  transfers between devices with their start and end apart: 2, of which 2 were waited for; matrix products, arithmetic and copies ran while one was open for 0% of the time, Pallas kernels for 0%

profile of v1, /device:TPU:8, one launch (start us, length us, event | category | flops | bytes accessed | tf_op | source)
XLA Modules:
  0.0 470.4 jit_solution(14678517795647706684)
XLA Ops:
  6.5 0.0 copy-start
  6.5 0.0 all-reduce.2.cloned.1.call-start
  6.5 1.1 stack.2
  7.6 0.0 copy-start.1
  7.6 119.6 %all_to_all.5 = bf16[64,16,1024]{2,1,0:T(8,128)(2,1)S(1)} all-to-all(bf16[64,16,1024]{2,1,0:T(8,128)(2,1)S(1)} %stack.2), channel_id=1, replica_groups=mesh['loop'=64,'narrow'=8] {'loop'}, dimensions={0} | all-to-all | bytes 4194304 | tf_op jit(solution)/shard_map/all_to_all | solution.py:10
  127.2 0.0 copy-done.1
  127.2 0.0 copy-start.2
  127.2 1.1 fusion.6
  128.4 0.0 copy-done.2
  128.4 1.1 fusion.5
  129.6 2.3 pad_maximum_fusion
  131.8 0.0 all-reduce.2.cloned.1.call-update
  131.9 0.0 reduce-scatter.2.cloned.1.call-start
  131.9 101.5 %all-reduce.2.cloned.1.call-done = f32[1024,896]{0,1:T(8,128)} async-done(((f32[1024,896]{0,1:T(8,128)}), f32[1024,896]{0,1:T(8,128)}) %all-reduce.2.cloned.1.call-update) | async-done | bytes 3670032 | tf_op jit(solution)/shard_map/psum | solution.py:19
  233.5 0.0 copy-done
  233.5 5.3 %fusion.1 = f32[1024,1024]{1,0:T(8,128)} fusion(bf16[448,1024]{1,0:T(8,128)(2,1)S(1)} %copy-done, f32[1024,896]{0,1:T(8,128)} %all-reduce.2.cloned.1.call-done), kind=kOutput, calls=%fused_computation.3 | convolution fusion | flops 942276608 | bytes 8781824 | tf_op jit(solution)/shard_map/dot_general | solution.py:22
  238.8 0.0 reduce-scatter.2.cloned.1.call-update
  238.8 223.3 %reduce-scatter.2.cloned.1.call-done = f32[16,1024]{1,0:T(8,128)} async-done(((f32[1024,1024]{1,0:T(8,128)}), f32[16,1024]{1,0:T(8,128)}) %reduce-scatter.2.cloned.1.call-update) | async-done | bytes 65552 | tf_op jit(solution)/shard_map/reduce_scatter | solution.py:21
  462.1 1.5 convert_element_type.7
Async XLA Ops:
  6.5 226.9 %copy-start = (bf16[448,1024]{1,0:T(8,128)(2,1)S(1)}, bf16[448,1024]{1,0:T(8,128)(2,1)}, u32[]{:S(2)}) copy-start(bf16[448,1024]{1,0:T(8,128)(2,1)} %param.7) | copy-start | bytes 2752516
  6.5 226.9 %all-reduce.2.cloned.1.call-start = ((), (), s32[]{:S(2)}) async-start(), calls=%async_computation.2 | async-start | bytes 7340032 | tf_op jit(solution)/shard_map/psum | solution.py:19
  7.6 119.6 %copy-start.1 = (bf16[1024,448]{0,1:T(8,128)(2,1)S(1)}, bf16[1024,448]{0,1:T(8,128)(2,1)}, u32[]{:S(2)}) copy-start(bf16[1024,448]{0,1:T(8,128)(2,1)} %param.6) | copy-start | bytes 2752516
  127.2 1.2 copy-start.2
  131.9 330.2 %reduce-scatter.2.cloned.1.call-start = ((), (), s32[]{:S(2)}) async-start(), calls=%async_computation.3 | async-start | bytes 4259840 | tf_op jit(solution)/shard_map/reduce_scatter | solution.py:21
Sparse Core Ops, SparseCore 0:
  132.0 101.4 all-reduce.1
  238.9 223.1 reduce-scatter.1

commit v2 on v0

--- a/solution.py
+++ b/solution.py
@@ -14,7 +14,7 @@
         ),
         axis=1,
     )
-    totals = lax.psum(partial_sums, "narrow")
+    totals = jnp.sum(lax.all_gather(partial_sums, "narrow"), axis=0)
     hidden = (jax.nn.silu(totals[:, :width]) * totals[:, width:]).astype(jnp.bfloat16)
     mixed = lax.psum_scatter(
         jnp.dot(hidden, down_weight, preferred_element_type=jnp.float32),

time: 507 us -> 729 us (1.44)
  waiting for transfers between devices: 480 us -> 664 us
  local copies, waits for them, and re-layouts: 0.01 us -> 30.8 us
  other arithmetic: 3.75 us -> 13.2 us
    all_gather x0 -> x1, waiting for transfers between devices: none -> 289 us  [shards(): totals = jnp.sum(lax.all_gather(partial_sums, 'narrow'), axis=0)]
    psum x1 -> x0, waiting for transfers between devices: 105 us -> none  [shards(): totals = lax.psum(partial_sums, 'narrow')]
    unnamed x6 -> x7, local copies, waits for them, and re-layouts: 0.01 us -> 30.8 us
    reduce_sum x0 -> x1, other arithmetic: none -> 9.43 us  [shards(): totals = jnp.sum(lax.all_gather(partial_sums, 'narrow'), axis=0)]
where the time goes in v2:
time: 729 us
  waiting for transfers between devices  664 us (91%)
  local copies, waits for them, and re-layouts  30.8 us (4%)
  other arithmetic  13.2 us (2%)
  between operations  13.2 us (2%)
  matrix products  7.56 us (1%)
    all_gather x1, waiting for transfers between devices, shards(): totals = jnp.sum(lax.all_gather(partial_sums, 'narrow'), axis=0)  289 us
    reduce_scatter x1, waiting for transfers between devices, shards(): lax.psum_scatter(jnp.dot(hidden, down_weight, preferred_element_type=jnp....  223 us
    all_gather x1, waiting for transfers between devices, shards(): block_rows = lax.all_gather(tokens, 'loop', axis=0, tiled=True)  152 us
    unnamed x7, local copies, waits for them, and re-layouts  30.8 us
  transfers between devices with their start and end apart: 3, of which 3 were waited for; matrix products, arithmetic and copies ran while one was open for 0% of the time, Pallas kernels for 0%

profile of v2, /device:TPU:8, one launch (start us, length us, event | category | flops | bytes accessed | tf_op | source)
XLA Modules:
  0.0 728.8 jit_solution(14918098127264116976)
XLA Ops:
  6.5 0.0 copy-start
  6.5 0.0 all-gather.4.cloned.1.call-start
  6.5 0.7 all-gather.4.cloned.1.call-update
  7.3 0.0 copy-start.2
  7.3 0.0 all-gather.6.cloned.1.call-start
  7.3 151.5 %all-gather.4.cloned.1.call-done = bf16[1024,1024]{1,0:T(8,128)(2,1)} async-done(((bf16[16,1024]{1,0:T(8,128)(2,1)}), bf16[1024,1024]{1,0:T(8,128)(2,1)}) %all-gather.4.cloned.1.call-update) | async-done | bytes 2097168 | tf_op jit(solution)/shard_map/all_gather | solution.py:9
  158.8 0.0 copy-start.1
  158.8 3.1 fusion.6
  162.0 0.0 copy-done.2
  162.0 0.0 copy-done.1
  162.0 1.2 fusion.5
  163.1 2.3 pad_maximum_fusion
  165.4 0.0 all-gather.6.cloned.1.call-update
  165.4 0.0 reduce-scatter.2.cloned.1.call-start
  165.5 288.5 %all-gather.6.cloned.1.call-done = f32[8192,896]{0,1:T(8,128)} async-done(((f32[1024,896]{0,1:T(8,128)}), f32[8192,896]{0,1:T(8,128)}) %all-gather.6.cloned.1.call-update) | async-done | bytes 29360144 | tf_op jit(solution)/shard_map/all_gather | solution.py:17
  454.0 30.8 %copy.5 = f32[112,8,8,1024]{3,2,1,0:T(8,128)S(1)} copy(f32[112,8,8,1024]{3,1,2,0:T(8,128)} %bitcast.10) | data formatting | bytes 58720256
  484.8 9.4 %bitcast_reduce_fusion = f32[1024,896]{0,1:T(8,128)S(1)} fusion(f32[112,8,8,1024]{3,2,1,0:T(8,128)S(1)} %copy.5), kind=kLoop, calls=%fused_computation | loop fusion | flops 6422528 | bytes 33030144 | tf_op jit(solution)/shard_map/reduce_sum | solution.py:17
  494.3 0.0 copy-done
  494.3 3.3 fusion.1
  497.6 0.0 reduce-scatter.2.cloned.1.call-update
  497.6 223.2 %reduce-scatter.2.cloned.1.call-done = f32[16,1024]{1,0:T(8,128)} async-done(((f32[1024,1024]{1,0:T(8,128)}), f32[16,1024]{1,0:T(8,128)}) %reduce-scatter.2.cloned.1.call-update) | async-done | bytes 65552 | tf_op jit(solution)/shard_map/reduce_scatter | solution.py:19
  720.8 1.5 convert_element_type.7
Async XLA Ops:
  6.5 487.7 %copy-start = (bf16[448,1024]{1,0:T(8,128)(2,1)S(1)}, bf16[448,1024]{1,0:T(8,128)(2,1)}, u32[]{:S(2)}) copy-start(bf16[448,1024]{1,0:T(8,128)(2,1)} %param.7) | copy-start | bytes 2752516
  6.5 152.3 %all-gather.4.cloned.1.call-start = ((), (), s32[]{:S(2)}) async-start(), calls=%async_computation.1 | async-start | bytes 2129920 | tf_op jit(solution)/shard_map/all_gather | solution.py:9
  7.3 154.7 %copy-start.2 = (bf16[1024,448]{0,1:T(8,128)(2,1)S(1)}, bf16[1024,448]{0,1:T(8,128)(2,1)}, u32[]{:S(2)}) copy-start(bf16[1024,448]{0,1:T(8,128)(2,1)} %param.5) | copy-start | bytes 2752516
  7.3 446.7 %all-gather.6.cloned.1.call-start = ((), (), s32[]{:S(2)}) async-start(), calls=%async_computation.3 | async-start | bytes 33030144 | tf_op jit(solution)/shard_map/all_gather | solution.py:17
  158.8 3.1 copy-start.1
  165.4 555.4 %reduce-scatter.2.cloned.1.call-start = ((), (), s32[]{:S(2)}) async-start(), calls=%async_computation.2 | async-start | bytes 4259840 | tf_op jit(solution)/shard_map/reduce_scatter | solution.py:19
Sparse Core Ops, SparseCore 0:
  10.7 148.1 all-gather.3
  165.6 288.4 all-gather.5
  497.7 223.0 reduce-scatter.1
